TPU v7x, 128 devices: a whole 4x4x4 slice. The times are simulated.
128 devices in a mesh: dp: 2 (over core), lat: 8 (over z, y_hi), lon: 8 (over y_lo, x).
Axes of the slice: x: 4, y: 4 (y_hi: 2, y_lo: 2; y = y_hi * 2 + y_lo), z: 4, core: 2. Of those that a mesh axis runs over, the one named last changes fastest.
Arguments:
- fields: bfloat16 [2, 640, 1024, 128], P('dp', 'lat', 'lon'), may hold values from -6 to 6
- down_weight: bfloat16 [3, 3, 128, 128], P(None, None, 'dp'), may hold values from -0.1875 to 0.1875
- mid_weight: bfloat16 [3, 3, 128, 128], P(None, None, 'dp'), may hold values from -0.1875 to 0.1875
- up_weight: bfloat16 [3, 3, 128, 128], P(None, None, 'dp'), may hold values from -0.1875 to 0.1875
- cotangent: bfloat16 [2, 640, 1024, 128], P('dp', 'lat', 'lon'), may hold values from -6 to 6
Outputs:
- level_out: bfloat16 [2, 640, 1024, 128], P('dp', 'lat', 'lon')
- grad_fields: bfloat16 [2, 640, 1024, 128], P('dp', 'lat', 'lon')
- grad_down: float32 [3, 3, 128, 128], P(None, None, 'dp')
- grad_mid: float32 [3, 3, 128, 128], P(None, None, 'dp')
- grad_up: float32 [3, 3, 128, 128], P(None, None, 'dp')
All inputs are finite; a program needn't handle non-finite values.
Results may differ from a plain program's by a relative error of at most 0.012.
Values may be sent and summed in bfloat16 or wider, within the bound.
No kernel may reach another device: no remote copies, remote signals or barrier semaphores. Data moves between devices by JAX's collectives and lax.ppermute only.
A program may use at most 128 MiB of HBM per device.

v0:
```python
import math
import jax
import jax.numpy as jnp
from jax import lax
from jax.sharding import PartitionSpec as P


def extended(block, sides, width, periodic):
    for axis, dim in sides:
        count = lax.axis_size(axis)
        forward = [(i, i + 1) for i in range(count - 1)]
        if periodic:
            forward.append((count - 1, 0))
        backward = [(target, source) for source, target in forward]
        low = lax.ppermute(
            lax.slice_in_dim(block, block.shape[dim] - width, None, axis=dim), axis, forward
        )
        high = lax.ppermute(lax.slice_in_dim(block, 0, width, axis=dim), axis, backward)
        block = jnp.concatenate([low, block, high], axis=dim)
    return block


def framed(field):
    tall = extended(field, (("lat", 1),), 1, False)
    return extended(tall, (("lon", 2),), 1, True)


def convolve(padded, kernel, stride, dilate, padding):
    return lax.conv_general_dilated(
        padded,
        kernel,
        (stride, stride),
        padding,
        lhs_dilation=(dilate, dilate),
        dimension_numbers=("NHWC", "HWIO", "NHWC"),
        preferred_element_type=jnp.float32,
    )


def taps_down(padded, kernel):
    return convolve(padded, kernel, 2, 1, "VALID")


def taps_same(padded, kernel):
    return convolve(padded, kernel, 1, 1, "VALID")


def taps_up(padded, kernel):
    return convolve(padded, kernel[::-1, ::-1], 1, 2, ((-1, 0), (-1, 0)))


def kernel_grad(padded, grad, dilate, layout):
    result = lax.conv_general_dilated(
        padded,
        grad,
        (1, 1),
        "VALID",
        rhs_dilation=(dilate, dilate),
        dimension_numbers=("CHWN", "IHWO", layout),
        preferred_element_type=jnp.float32,
    )
    return result[:3, :3]


def swap_io(kernel):
    return jnp.transpose(kernel, (0, 1, 3, 2))


def body(fields, down_weight, mid_weight, up_weight, cotangent):
    kernel_down, kernel_mid, kernel_up = (
        lax.all_gather(down_weight, "dp", axis=2, tiled=True),
        lax.all_gather(mid_weight, "dp", axis=2, tiled=True),
        lax.all_gather(up_weight, "dp", axis=2, tiled=True),
    )
    cells = (
        fields.shape[0]
        * lax.axis_size("dp")
        * fields.shape[1]
        * lax.axis_size("lat")
        * fields.shape[2]
        * lax.axis_size("lon")
    )
    scale = 1.0 / math.sqrt(cells)
    framed_in = framed(fields)
    down = taps_down(framed_in, kernel_down).astype(jnp.bfloat16)
    framed_down = framed(down)
    pre = taps_same(framed_down, kernel_mid)
    mid = jax.nn.silu(pre).astype(jnp.bfloat16)
    framed_mid = framed(mid)
    level_out = (fields.astype(jnp.float32) + taps_up(framed_mid, kernel_up)).astype(jnp.bfloat16)
    framed_cot = framed(cotangent)
    up_term = kernel_grad(framed_cot, mid, 2, "HWCN") * scale
    grad_mid_map = taps_down(framed_cot, swap_io(kernel_up))
    sig = jax.nn.sigmoid(pre)
    grad_pre = (grad_mid_map * sig * (1.0 + pre * (1.0 - sig))).astype(jnp.bfloat16)
    mid_term = kernel_grad(framed_down, grad_pre, 1, "HWNC") * scale
    grad_down_map = taps_same(framed(grad_pre), swap_io(kernel_mid)[::-1, ::-1]).astype(
        jnp.bfloat16
    )
    down_term = kernel_grad(framed_in, grad_down_map, 2, "HWNC") * scale
    grad_fields = (
        cotangent.astype(jnp.float32) + taps_up(framed(grad_down_map), swap_io(kernel_down))
    ).astype(jnp.bfloat16)
    totals = lax.psum((down_term, mid_term, up_term), ("lat", "lon"))
    grad_down, grad_mid, grad_up = (
        lax.psum_scatter(
            totals[0].astype(jnp.bfloat16), "dp", scatter_dimension=2, tiled=True
        ).astype(jnp.float32),
        lax.psum_scatter(
            totals[1].astype(jnp.bfloat16), "dp", scatter_dimension=2, tiled=True
        ).astype(jnp.float32),
        lax.psum_scatter(
            totals[2].astype(jnp.bfloat16), "dp", scatter_dimension=2, tiled=True
        ).astype(jnp.float32),
    )
    return (level_out, grad_fields, grad_down, grad_mid, grad_up)


def solution(mesh):
    in_specs = (
        P("dp", "lat", "lon", None),
        P(None, None, "dp", None),
        P(None, None, "dp", None),
        P(None, None, "dp", None),
        P("dp", "lat", "lon", None),
    )
    out_specs = (
        P("dp", "lat", "lon", None),
        P("dp", "lat", "lon", None),
        P(None, None, "dp", None),
        P(None, None, "dp", None),
        P(None, None, "dp", None),
    )
    return jax.shard_map(body, mesh=mesh, in_specs=in_specs, out_specs=out_specs, check_vma=False)
```

profile of v0, /device:TPU:16, one launch (start us, length us, event | category | flops | bytes accessed | tf_op | source)
XLA Modules:
  0.0 591.8 jit_solution(1721154471314080505)
XLA Ops:
  10.2 6.1 %collective-permute-start = (bf16[1,1,128,128]{3,2,1,0:T(8,128)(2,1)S(1)}, bf16[1,1,128,128]{3,2,1,0:T(8,128)(2,1)S(1)}, u32[]{:S(2)}, u32[]{:S(2)}) collective-permute-start(bf16[1,1,128,128]{3,2,1,0:T(8,128)(2,1)S(1)} %get-tuple-element.33), channel_id=1, source_target_pairs={{0,8},{8,16},{16,24},{24,32},{32,40},{40,48},{48,56},{1,9},{9,17},... | collective-permute-start | bytes 98312 | tf_op jit(solution)/shard_map/ppermute | solution.py:15
  18.9 6.3 %collective-permute-start.12 = (bf16[1,1,128,128]{3,2,1,0:T(8,128)(2,1)S(1)}, bf16[1,1,128,128]{3,2,1,0:T(8,128)(2,1)S(1)}, u32[]{:S(2)}, u32[]{:S(2)}) collective-permute-start(bf16[1,1,128,128]{3,2,1,0:T(8,128)(2,1)S(1)} %get-tuple-element.31), channel_id=1, source_target_pairs={{0,8},{8,16},{16,24},{24,32},{32,40},{40,48},{48,56},{1,9},{9,17},... | collective-permute-start | bytes 98312 | tf_op jit(solution)/shard_map/ppermute | solution.py:15
  27.6 3.7 all_gather.10
  31.3 3.9 all_gather.11
  39.6 2.6 collective-permute-start.3
  42.4 4.6 collective-permute-start.15
  63.9 5.1 collective-permute-start.5
  69.1 4.4 fusion.132
  80.8 4.1 collective-permute-start.7
  103.5 3.3 collective-permute-start.8
  106.8 4.6 collective-permute-start.9
  114.1 3.6 collective-permute-start.16
  117.8 4.1 collective-permute-start.17
  123.1 5.3 fusion.79
  131.0 4.1 collective-permute-start.19
  140.6 3.6 fusion.76
  144.2 346.6 %all-reduce.2 = (bf16[3,3,128,128]{3,2,1,0:T(8,128)(2,1)}, bf16[3,3,128,128]{3,2,1,0:T(8,128)(2,1)}, bf16[3,3,128,128]{3,2,1,0:T(8,128)(2,1)}) all-reduce(f32[3,3,128,128]{3,2,1,0:T(8,128)} %fusion.76, f32[3,3,128,128]{3,2,1,0:T(8,128)S(1)} %copy-done.25, ...), channel_id=1, replica_groups=mesh['dp'=2,'lat'=8,'lon'=8] {'lat','lon'}, use_global_device_ids=true, to_apply=%region_0.1 | all-reduce | flops 442368 | bytes 2654208 | tf_op jit(solution)/shard_map/psum | solution.py:104
  492.8 4.1 collective-permute-start.11
  500.2 22.3 %collective-permute-start.21 = (bf16[1,1,64,128]{3,0,2,1:T(2,128)(2,1)S(1)}, bf16[1,1,64,128]{3,0,2,1:T(2,128)(2,1)S(1)}, u32[]{:S(2)}, u32[]{:S(2)}) collective-permute-start(bf16[1,1,64,128]{3,0,2,1:T(2,128)(2,1)S(1)} %slice.175), channel_id=1, source_target_pairs={{8,0},{16,8},{24,16},{32,24},{40,32},{48,40},{56,48},{9,1},{17,9},... | collective-permute-start | bytes 49160 | tf_op jit(solution)/shard_map/ppermute | solution.py:18
  522.7 3.7 pad_maximum_fusion.15
  529.1 3.2 collective-permute-start.23
  532.3 20.0 %fusion.21 = bf16[1,80,128,128]{3,0,2,1:T(2,128)(2,1)S(1)} fusion(bf16[1,80,128,128]{3,2,1,0:T(8,128)(2,1)S(1)} %copy-done.12, bf16[3,3,128,128]{3,2,1,0:T(8,128)(2,1)S(1)} %copy-done.29, bf16[1,42,66,128]{3,0,2,1:T(2,128)(2,1)S(1)} %pad_maximum_fusion.15), kind=kOutput, calls=%fused_computation.25 | convolution fusion | flops 758906880 | bytes 6247424 | tf_op jit(solution)/shard_map/conv_general_dilated | solution.py:29
  554.4 3.7 pad_maximum_fusion.14
  558.1 20.0 %fusion.19 = bf16[1,80,128,128]{3,0,2,1:T(2,128)(2,1)S(1)} fusion(bf16[1,80,128,128]{3,2,1,0:T(8,128)(2,1)S(1)} %copy-done.14, bf16[3,3,128,128]{3,2,1,0:T(8,128)(2,1)S(1)} %copy-done.27, bf16[1,42,66,128]{3,0,2,1:T(2,128)(2,1)S(1)} %pad_maximum_fusion.14), kind=kOutput, calls=%fused_computation.22 | convolution fusion | flops 758906880 | bytes 6247424 | tf_op jit(solution)/shard_map/conv_general_dilated | solution.py:29
  (213 shorter events, 83.6 us)
Async XLA Ops:
  7.2 572.9 %reduce-scatter.8.cloned.1.call-start = ((), (), s32[]{:S(2)}) async-start(), calls=%async_computation.5 | async-start | bytes 442368 | tf_op jit(solution)/shard_map/reduce_scatter | solution.py:112
  8.0 29.6 %collective-permute-start.1 = (bf16[1,1,128,128]{3,2,1,0:T(8,128)(2,1)S(1)}, bf16[1,1,128,128]{3,2,1,0:T(8,128)(2,1)S(1)}, u32[]{:S(2)}, u32[]{:S(2)}) collective-permute-start(bf16[1,1,128,128]{3,2,1,0:T(8,128)(2,1)S(1)} %get-tuple-element.32), channel_id=1, source_target_pairs={{8,0},{16,8},{24,16},{32,24},{40,32},{48,40},{56,48},{9,1},{17,9},... | collective-permute-start | bytes 98312 | tf_op jit(solution)/shard_map/ppermute | solution.py:18
  10.2 25.0 %collective-permute-start = (bf16[1,1,128,128]{3,2,1,0:T(8,128)(2,1)S(1)}, bf16[1,1,128,128]{3,2,1,0:T(8,128)(2,1)S(1)}, u32[]{:S(2)}, u32[]{:S(2)}) collective-permute-start(bf16[1,1,128,128]{3,2,1,0:T(8,128)(2,1)S(1)} %get-tuple-element.33), channel_id=1, source_target_pairs={{0,8},{8,16},{16,24},{24,32},{32,40},{40,48},{48,56},{1,9},{9,17},... | collective-permute-start | bytes 98312 | tf_op jit(solution)/shard_map/ppermute | solution.py:15
  17.0 25.2 %collective-permute-start.13 = (bf16[1,1,128,128]{3,2,1,0:T(8,128)(2,1)S(1)}, bf16[1,1,128,128]{3,2,1,0:T(8,128)(2,1)S(1)}, u32[]{:S(2)}, u32[]{:S(2)}) collective-permute-start(bf16[1,1,128,128]{3,2,1,0:T(8,128)(2,1)S(1)} %get-tuple-element.30), channel_id=1, source_target_pairs={{8,0},{16,8},{24,16},{32,24},{40,32},{48,40},{56,48},{9,1},{17,9},... | collective-permute-start | bytes 98312 | tf_op jit(solution)/shard_map/ppermute | solution.py:18
  18.9 18.7 %collective-permute-start.12 = (bf16[1,1,128,128]{3,2,1,0:T(8,128)(2,1)S(1)}, bf16[1,1,128,128]{3,2,1,0:T(8,128)(2,1)S(1)}, u32[]{:S(2)}, u32[]{:S(2)}) collective-permute-start(bf16[1,1,128,128]{3,2,1,0:T(8,128)(2,1)S(1)} %get-tuple-element.31), channel_id=1, source_target_pairs={{0,8},{8,16},{16,24},{24,32},{32,40},{40,48},{48,56},{1,9},{9,17},... | collective-permute-start | bytes 98312 | tf_op jit(solution)/shard_map/ppermute | solution.py:15
  38.0 8.9 %collective-permute-start.2 = (bf16[1,82,1,128]{3,2,1,0:T(2,128)(2,1)S(1)}, bf16[1,82,1,128]{3,2,1,0:T(2,128)(2,1)S(1)}, u32[]{:S(2)}, u32[]{:S(2)}) collective-permute-start(bf16[1,82,1,128]{3,2,1,0:T(2,128)(2,1)S(1)} %get-tuple-element.28), channel_id=1, source_target_pairs={{0,1},{1,2},{2,3},{3,4},{4,5},{5,6},{6,7},{7,0},{8,9},{9,10},{10,1... | collective-permute-start | bytes 62984 | tf_op jit(solution)/shard_map/ppermute | solution.py:15
  42.3 11.2 %collective-permute-start.14 = (bf16[1,82,1,128]{3,2,1,0:T(2,128)(2,1)S(1)}, bf16[1,82,1,128]{3,2,1,0:T(2,128)(2,1)S(1)}, u32[]{:S(2)}, u32[]{:S(2)}) collective-permute-start(bf16[1,82,1,128]{3,2,1,0:T(2,128)(2,1)S(1)} %get-tuple-element.26), channel_id=1, source_target_pairs={{0,1},{1,2},{2,3},{3,4},{4,5},{5,6},{6,7},{7,0},{8,9},{9,10},{10,1... | collective-permute-start | bytes 62984 | tf_op jit(solution)/shard_map/ppermute | solution.py:15
  42.4 11.1 %collective-permute-start.15 = (bf16[1,82,1,128]{3,2,1,0:T(2,128)(2,1)S(1)}, bf16[1,82,1,128]{3,2,1,0:T(2,128)(2,1)S(1)}, u32[]{:S(2)}, u32[]{:S(2)}) collective-permute-start(bf16[1,82,1,128]{3,2,1,0:T(2,128)(2,1)S(1)} %get-tuple-element.27), channel_id=1, source_target_pairs={{1,0},{2,1},{3,2},{4,3},{5,4},{6,5},{7,6},{0,7},{9,8},{10,9},{11,1... | collective-permute-start | bytes 62984 | tf_op jit(solution)/shard_map/ppermute | solution.py:18
  61.5 18.3 %collective-permute-start.4 = (bf16[1,1,64,128]{3,2,1,0:T(8,128)(2,1)S(1)}, bf16[1,1,64,128]{3,2,1,0:T(8,128)(2,1)S(1)}, u32[]{:S(2)}, u32[]{:S(2)}) collective-permute-start(bf16[1,1,64,128]{3,2,1,0:T(8,128)(2,1)S(1)} %slice.150), channel_id=1, source_target_pairs={{0,8},{8,16},{16,24},{24,32},{32,40},{40,48},{48,56},{1,9},{9,17},... | collective-permute-start | bytes 49160 | tf_op jit(solution)/shard_map/ppermute | solution.py:15
  63.9 15.9 %collective-permute-start.5 = (bf16[1,1,64,128]{3,1,2,0:T(2,128)(2,1)S(1)}, bf16[1,1,64,128]{3,1,2,0:T(2,128)(2,1)S(1)}, u32[]{:S(2)}, u32[]{:S(2)}) collective-permute-start(bf16[1,1,64,128]{3,1,2,0:T(2,128)(2,1)S(1)} %slice.153), channel_id=1, source_target_pairs={{8,0},{16,8},{24,16},{32,24},{40,32},{48,40},{56,48},{9,1},{17,9},... | collective-permute-start | bytes 49160 | tf_op jit(solution)/shard_map/ppermute | solution.py:18
  80.7 10.4 %collective-permute-start.6 = (bf16[1,42,1,128]{3,1,2,0:T(8,128)(2,1)S(1)}, bf16[1,42,1,128]{3,1,2,0:T(8,128)(2,1)S(1)}, u32[]{:S(2)}, u32[]{:S(2)}) collective-permute-start(bf16[1,42,1,128]{3,1,2,0:T(8,128)(2,1)S(1)} %get-tuple-element.52), channel_id=1, source_target_pairs={{0,1},{1,2},{2,3},{3,4},{4,5},{5,6},{6,7},{7,0},{8,9},{9,10},{10,1... | collective-permute-start | bytes 32264 | tf_op jit(solution)/shard_map/ppermute | solution.py:15
  80.8 10.3 %collective-permute-start.7 = (bf16[1,42,1,128]{3,1,2,0:T(8,128)(2,1)S(1)}, bf16[1,42,1,128]{3,1,2,0:T(8,128)(2,1)S(1)}, u32[]{:S(2)}, u32[]{:S(2)}) collective-permute-start(bf16[1,42,1,128]{3,1,2,0:T(8,128)(2,1)S(1)} %get-tuple-element.53), channel_id=1, source_target_pairs={{1,0},{2,1},{3,2},{4,3},{5,4},{6,5},{7,6},{0,7},{9,8},{10,9},{11,1... | collective-permute-start | bytes 32264 | tf_op jit(solution)/shard_map/ppermute | solution.py:18
  103.5 31.6 %collective-permute-start.8 = (bf16[1,1,64,128]{3,0,2,1:T(2,128)(2,1)}, bf16[1,1,64,128]{3,0,2,1:T(2,128)(2,1)}, u32[]{:S(2)}, u32[]{:S(2)}) collective-permute-start(bf16[1,1,64,128]{3,0,2,1:T(2,128)(2,1)} %slice.156), channel_id=1, source_target_pairs={{0,8},{8,16},{16,24},{24,32},{32,40},{40,48},{48,56},{1,9},{9,17},... | collective-permute-start | bytes 49160 | tf_op jit(solution)/shard_map/ppermute | solution.py:15
  106.8 385.8 %collective-permute-start.9 = (bf16[1,1,64,128]{3,0,2,1:T(2,128)(2,1)}, bf16[1,1,64,128]{3,0,2,1:T(2,128)(2,1)S(1)}, u32[]{:S(2)}, u32[]{:S(2)}) collective-permute-start(bf16[1,1,64,128]{3,0,2,1:T(2,128)(2,1)} %slice.159), channel_id=1, source_target_pairs={{8,0},{16,8},{24,16},{32,24},{40,32},{48,40},{56,48},{9,1},{17,9},... | collective-permute-start | bytes 49160 | tf_op jit(solution)/shard_map/ppermute | solution.py:18
  114.1 16.7 %collective-permute-start.16 = (bf16[1,1,64,128]{3,2,1,0:T(8,128)(2,1)}, bf16[1,1,64,128]{3,2,1,0:T(8,128)(2,1)S(1)}, u32[]{:S(2)}, u32[]{:S(2)}) collective-permute-start(bf16[1,1,64,128]{3,2,1,0:T(8,128)(2,1)} %slice.166), channel_id=1, source_target_pairs={{0,8},{8,16},{16,24},{24,32},{32,40},{40,48},{48,56},{1,9},{9,17},... | collective-permute-start | bytes 49160 | tf_op jit(solution)/shard_map/ppermute | solution.py:15
  117.8 13.1 %collective-permute-start.17 = (bf16[1,1,64,128]{3,1,2,0:T(2,128)(2,1)S(1)}, bf16[1,1,64,128]{3,1,2,0:T(2,128)(2,1)S(1)}, u32[]{:S(2)}, u32[]{:S(2)}) collective-permute-start(bf16[1,1,64,128]{3,1,2,0:T(2,128)(2,1)S(1)} %slice.169), channel_id=1, source_target_pairs={{8,0},{16,8},{24,16},{32,24},{40,32},{48,40},{56,48},{9,1},{17,9},... | collective-permute-start | bytes 49160 | tf_op jit(solution)/shard_map/ppermute | solution.py:18
  490.9 90.9 %reduce-scatter.6.cloned.1.call-start = ((), (), s32[]{:S(2)}) async-start(), calls=%async_computation.4 | async-start | bytes 442368 | tf_op jit(solution)/shard_map/reduce_scatter | solution.py:109
  492.7 30.0 %collective-permute-start.10 = (bf16[1,42,1,128]{3,0,2,1:T(2,128)(2,1)S(1)}, bf16[1,42,1,128]{3,0,2,1:T(2,128)(2,1)}, u32[]{:S(2)}, u32[]{:S(2)}) collective-permute-start(bf16[1,42,1,128]{3,0,2,1:T(2,128)(2,1)S(1)} %get-tuple-element.36), channel_id=1, source_target_pairs={{0,1},{1,2},{2,3},{3,4},{4,5},{5,6},{6,7},{7,0},{8,9},{9,10},{10,1... | collective-permute-start | bytes 32264 | tf_op jit(solution)/shard_map/ppermute | solution.py:15
  492.8 29.9 %collective-permute-start.11 = (bf16[1,42,1,128]{3,0,2,1:T(2,128)(2,1)S(1)}, bf16[1,42,1,128]{3,0,2,1:T(2,128)(2,1)}, u32[]{:S(2)}, u32[]{:S(2)}) collective-permute-start(bf16[1,42,1,128]{3,0,2,1:T(2,128)(2,1)S(1)} %get-tuple-element.37), channel_id=1, source_target_pairs={{1,0},{2,1},{3,2},{4,3},{5,4},{6,5},{7,6},{0,7},{9,8},{10,9},{11,1... | collective-permute-start | bytes 32264 | tf_op jit(solution)/shard_map/ppermute | solution.py:18
  498.3 28.1 %collective-permute-start.20 = (bf16[1,1,64,128]{3,0,2,1:T(2,128)(2,1)S(1)}, bf16[1,1,64,128]{3,0,2,1:T(2,128)(2,1)S(1)}, u32[]{:S(2)}, u32[]{:S(2)}) collective-permute-start(bf16[1,1,64,128]{3,0,2,1:T(2,128)(2,1)S(1)} %slice.172), channel_id=1, source_target_pairs={{0,8},{8,16},{16,24},{24,32},{32,40},{40,48},{48,56},{1,9},{9,17},... | collective-permute-start | bytes 49160 | tf_op jit(solution)/shard_map/ppermute | solution.py:15
  500.2 27.7 %collective-permute-start.21 = (bf16[1,1,64,128]{3,0,2,1:T(2,128)(2,1)S(1)}, bf16[1,1,64,128]{3,0,2,1:T(2,128)(2,1)S(1)}, u32[]{:S(2)}, u32[]{:S(2)}) collective-permute-start(bf16[1,1,64,128]{3,0,2,1:T(2,128)(2,1)S(1)} %slice.175), channel_id=1, source_target_pairs={{8,0},{16,8},{24,16},{32,24},{40,32},{48,40},{56,48},{9,1},{17,9},... | collective-permute-start | bytes 49160 | tf_op jit(solution)/shard_map/ppermute | solution.py:18
  522.6 60.8 %reduce-scatter.4.cloned.1.call-start = ((), (), s32[]{:S(2)}) async-start(), calls=%async_computation.3 | async-start | bytes 442368 | tf_op jit(solution)/shard_map/reduce_scatter | solution.py:106
  528.1 26.3 %collective-permute-start.22 = (bf16[1,42,1,128]{3,0,2,1:T(2,128)(2,1)S(1)}, bf16[1,42,1,128]{3,0,2,1:T(2,128)(2,1)S(1)}, u32[]{:S(2)}, u32[]{:S(2)}) collective-permute-start(bf16[1,42,1,128]{3,0,2,1:T(2,128)(2,1)S(1)} %get-tuple-element.34), channel_id=1, source_target_pairs={{0,1},{1,2},{2,3},{3,4},{4,5},{5,6},{6,7},{7,0},{8,9},{9,10},{10,1... | collective-permute-start | bytes 32264 | tf_op jit(solution)/shard_map/ppermute | solution.py:15
  529.1 25.3 %collective-permute-start.23 = (bf16[1,42,1,128]{3,0,2,1:T(2,128)(2,1)S(1)}, bf16[1,42,1,128]{3,0,2,1:T(2,128)(2,1)S(1)}, u32[]{:S(2)}, u32[]{:S(2)}) collective-permute-start(bf16[1,42,1,128]{3,0,2,1:T(2,128)(2,1)S(1)} %get-tuple-element.35), channel_id=1, source_target_pairs={{1,0},{2,1},{3,2},{4,3},{5,4},{6,5},{7,6},{0,7},{9,8},{10,9},{11,1... | collective-permute-start | bytes 32264 | tf_op jit(solution)/shard_map/ppermute | solution.py:18
  (37 other events, 882.8 us)
Sparse Core Ops, SparseCore 0:
  491.0 25.6 reduce-scatter.7
  522.7 8.5 reduce-scatter.5
  554.5 6.6 reduce-scatter.3
where the time goes:
time: 596 us; the launch traced here: 592 us
  blocking collectives  357 us (60%)
  starting transfers between devices  88.9 us (15%)
  matrix products  59.4 us (10%)
  local copies, waits for them, and re-layouts  41.8 us (7%)
  other arithmetic  29.3 us (5%)
  between operations  14.9 us (2%)
    psum x1, blocking collectives, body(): totals = lax.psum((down_term, mid_term, up_term), ('lat', 'lon'))  347 us
    ppermute x12, starting transfers between devices, extended(): lax.ppermute(lax.slice_in_dim(block, 0, width, axis=dim), axis, backward)  63.1 us
    conv_general_dilated x6, matrix products, convolve(): lax.conv_general_dilated(padded, kernel, (stride, stride), padding, lhs_d...  48.2 us
    ppermute x12, starting transfers between devices, extended(): lax.ppermute(lax.slice_in_dim(block, block.shape[dim] - width, None, axis...  25.5 us
    concatenate x10, other arithmetic, extended(): block = jnp.concatenate([low, block, high], axis=dim)  17 us
    unnamed x76, local copies, waits for them, and re-layouts  16.7 us
    concatenate x22, local copies, waits for them, and re-layouts, extended(): block = jnp.concatenate([low, block, high], axis=dim)  12.3 us
  transfers between devices with their start and end apart: 27, of which 1 were waited for; matrix products, arithmetic and copies ran while one was open for 17% of the time, Pallas kernels for 0%

commit v1 on v0

--- a/solution.py
+++ b/solution.py
@@ -1,8 +1,18 @@
+import functools
 import math
 import jax
 import jax.numpy as jnp
 from jax import lax
 from jax.sharding import PartitionSpec as P
+
+
+def divide_series_all(q_in, ax_name, bus_axis):
+    for c in (ax_name, bus_axis):
+        q_in = lax.psum(q_in, c)
+    return q_in
+
+
+review_roads = functools.partial(divide_series_all, ax_name="lon", bus_axis="lat")
 
 
 def extended(block, sides, width, periodic):
@@ -101,7 +111,7 @@
     grad_fields = (
         cotangent.astype(jnp.float32) + taps_up(framed(grad_down_map), swap_io(kernel_down))
     ).astype(jnp.bfloat16)
-    totals = lax.psum((down_term, mid_term, up_term), ("lat", "lon"))
+    totals = review_roads((down_term, mid_term, up_term))
     grad_down, grad_mid, grad_up = (
         lax.psum_scatter(
             totals[0].astype(jnp.bfloat16), "dp", scatter_dimension=2, tiled=True

time: 596 us -> 392 us (0.66)
  blocking collectives: 357 us -> 99.6 us
  waiting for transfers between devices: 0.98 us -> 64.5 us
  starting transfers between devices: 88.9 us -> 73 us
    psum x1, blocking collectives: 347 us -> 89.8 us  [divide_series_all(): q_in = lax.psum(q_in, c)]
    psum x0 -> x1, waiting for transfers between devices: none -> 62.8 us  [divide_series_all(): q_in = lax.psum(q_in, c)]
    ppermute x12, starting transfers between devices: 63.1 us -> 42.2 us  [extended(): lax.ppermute(lax.slice_in_dim(block, 0, width, axis=dim), axis, backward)]
    unnamed x76 -> x72, local copies, waits for them, and re-layouts: 16.7 us -> 18.5 us
  transfers between devices with their start and end apart: 27 -> 28, of which waited for: 1 -> 2; matrix products, arithmetic and copies ran while one was open for 17% -> 27% of each run, Pallas kernels for 0% -> 0%
where the time goes in v1:
time: 392 us; the launch traced here: 385 us
  blocking collectives  99.6 us (25%)
  starting transfers between devices  73 us (19%)
  waiting for transfers between devices  64.5 us (16%)
  matrix products  61.1 us (16%)
  local copies, waits for them, and re-layouts  44 us (11%)
  other arithmetic  27.8 us (7%)
  between operations  14.9 us (4%)
    psum x1, blocking collectives, divide_series_all(): q_in = lax.psum(q_in, c)  89.8 us
    psum x1, waiting for transfers between devices, divide_series_all(): q_in = lax.psum(q_in, c)  62.8 us
    conv_general_dilated x6, matrix products, convolve(): lax.conv_general_dilated(padded, kernel, (stride, stride), padding, lhs_d...  49.9 us
    ppermute x12, starting transfers between devices, extended(): lax.ppermute(lax.slice_in_dim(block, 0, width, axis=dim), axis, backward)  42.2 us
    ppermute x12, starting transfers between devices, extended(): lax.ppermute(lax.slice_in_dim(block, block.shape[dim] - width, None, axis...  30.7 us
    unnamed x72, local copies, waits for them, and re-layouts  18.5 us
    concatenate x10, other arithmetic, extended(): block = jnp.concatenate([low, block, high], axis=dim)  16.8 us
    concatenate x22, local copies, waits for them, and re-layouts, extended(): block = jnp.concatenate([low, block, high], axis=dim)  13 us
  transfers between devices with their start and end apart: 28, of which 2 were waited for; matrix products, arithmetic and copies ran while one was open for 27% of the time, Pallas kernels for 0%

profile of v1, /device:TPU:16, one launch (start us, length us, event | category | flops | bytes accessed | tf_op | source)
XLA Modules:
  0.0 384.9 jit_solution(6935250728537598364)
XLA Ops:
  10.2 6.1 %collective-permute-start = (bf16[1,1,128,128]{3,2,1,0:T(8,128)(2,1)S(1)}, bf16[1,1,128,128]{3,2,1,0:T(8,128)(2,1)S(1)}, u32[]{:S(2)}, u32[]{:S(2)}) collective-permute-start(bf16[1,1,128,128]{3,2,1,0:T(8,128)(2,1)S(1)} %get-tuple-element.36), channel_id=1, source_target_pairs={{0,8},{8,16},{16,24},{24,32},{32,40},{40,48},{48,56},{1,9},{9,17},... | collective-permute-start | bytes 98312 | tf_op jit(solution)/shard_map/ppermute | solution.py:25
  18.9 6.3 %collective-permute-start.12 = (bf16[1,1,128,128]{3,2,1,0:T(8,128)(2,1)S(1)}, bf16[1,1,128,128]{3,2,1,0:T(8,128)(2,1)S(1)}, u32[]{:S(2)}, u32[]{:S(2)}) collective-permute-start(bf16[1,1,128,128]{3,2,1,0:T(8,128)(2,1)S(1)} %get-tuple-element.34), channel_id=1, source_target_pairs={{0,8},{8,16},{16,24},{24,32},{32,40},{40,48},{48,56},{1,9},{9,17},... | collective-permute-start | bytes 98312 | tf_op jit(solution)/shard_map/ppermute | solution.py:25
  27.6 3.7 all_gather.10
  31.3 3.8 all_gather.11
  42.4 4.6 %collective-permute-start.15 = (bf16[1,82,1,128]{3,2,1,0:T(2,128)(2,1)S(1)}, bf16[1,82,1,128]{3,2,1,0:T(2,128)(2,1)S(1)}, u32[]{:S(2)}, u32[]{:S(2)}) collective-permute-start(bf16[1,82,1,128]{3,2,1,0:T(2,128)(2,1)S(1)} %get-tuple-element.30), channel_id=1, source_target_pairs={{1,0},{2,1},{3,2},{4,3},{5,4},{6,5},{7,6},{0,7},{9,8},{10,9},{11,1... | collective-permute-start | bytes 62984 | tf_op jit(solution)/shard_map/ppermute | solution.py:28
  64.0 5.1 %collective-permute-start.5 = (bf16[1,1,64,128]{3,1,2,0:T(2,128)(2,1)S(1)}, bf16[1,1,64,128]{3,1,2,0:T(2,128)(2,1)S(1)}, u32[]{:S(2)}, u32[]{:S(2)}) collective-permute-start(bf16[1,1,64,128]{3,1,2,0:T(2,128)(2,1)S(1)} %slice.153), channel_id=1, source_target_pairs={{8,0},{16,8},{24,16},{32,24},{40,32},{48,40},{56,48},{9,1},{17,9},... | collective-permute-start | bytes 49160 | tf_op jit(solution)/shard_map/ppermute | solution.py:28
  69.1 4.3 %fusion.132 = (bf16[82,8,18,128,1]{3,1,4,2,0:T(8,128)(2,1)}, bf16[82,1,8,18,128]{4,2,3,0,1:T(8,128)(2,1)S(1)}) fusion(bf16[82,1,7,1,128]{4,2,3,0,1:T(8,128)(2,1)} %get-tuple-element.23, bf16[82,1,8,17,128]{4,2,3,0,1:T(8,128)(2,1)} %slice.186), kind=kLoop, calls=%fused_computation.152 | loop fusion | flops 9068544 | bytes 9047552 | tf_op jit(solution)/shard_map/concatenate | solution.py:29
  80.7 4.1 %collective-permute-start.7 = (bf16[1,42,1,128]{3,1,2,0:T(8,128)(2,1)S(1)}, bf16[1,42,1,128]{3,1,2,0:T(8,128)(2,1)S(1)}, u32[]{:S(2)}, u32[]{:S(2)}) collective-permute-start(bf16[1,42,1,128]{3,1,2,0:T(8,128)(2,1)S(1)} %get-tuple-element.56), channel_id=1, source_target_pairs={{1,0},{2,1},{3,2},{4,3},{5,4},{6,5},{7,6},{0,7},{9,8},{10,9},{11,1... | collective-permute-start | bytes 32264 | tf_op jit(solution)/shard_map/ppermute | solution.py:28
  103.6 3.3 collective-permute-start.8
  106.9 4.6 %collective-permute-start.9 = (bf16[1,1,64,128]{3,0,2,1:T(2,128)(2,1)}, bf16[1,1,64,128]{3,0,2,1:T(2,128)(2,1)S(1)}, u32[]{:S(2)}, u32[]{:S(2)}) collective-permute-start(bf16[1,1,64,128]{3,0,2,1:T(2,128)(2,1)} %slice.159), channel_id=1, source_target_pairs={{8,0},{16,8},{24,16},{32,24},{40,32},{48,40},{56,48},{9,1},{17,9},... | collective-permute-start | bytes 49160 | tf_op jit(solution)/shard_map/ppermute | solution.py:28
  112.2 3.6 collective-permute-start.16
  115.9 4.1 %collective-permute-start.17 = (bf16[1,1,64,128]{3,1,2,0:T(2,128)(2,1)S(1)}, bf16[1,1,64,128]{3,1,2,0:T(2,128)(2,1)S(1)}, u32[]{:S(2)}, u32[]{:S(2)}) collective-permute-start(bf16[1,1,64,128]{3,1,2,0:T(2,128)(2,1)S(1)} %slice.169), channel_id=1, source_target_pairs={{8,0},{16,8},{24,16},{32,24},{40,32},{48,40},{56,48},{9,1},{17,9},... | collective-permute-start | bytes 49160 | tf_op jit(solution)/shard_map/ppermute | solution.py:28
  121.2 5.3 %fusion.79 = f32[3,3,128,128]{3,2,1,0:T(8,128)} fusion(bf16[42,8,9,128,1]{3,1,4,2,0:T(8,128)(2,1)S(1)} %fusion.96, bf16[42,8,9,128,1]{3,1,4,2,0:T(8,128)(2,1)} %get-tuple-element.41, bf16[42,8,9,128,1]{3,1,4,2,0:T(8,128)(2,1)} %copy.67, bf16[40,8,9,128]{3,1,2,0:T(8,128)(2,1)} %copy-done.20, pred[8,9]{0,1:T(8,128)(4,1)S(1)} %copy-done.29), kind=kOutput, calls=%fused_computation.81 | convolution fusion | flops 852185088 | bytes 3649608 | tf_op jit(solution)/shard_map/conv_general_dilated | solution.py:63
  129.0 4.1 %collective-permute-start.19 = (bf16[1,42,1,128]{3,1,2,0:T(8,128)(2,1)S(1)}, bf16[1,42,1,128]{3,1,2,0:T(8,128)(2,1)S(1)}, u32[]{:S(2)}, u32[]{:S(2)}) collective-permute-start(bf16[1,42,1,128]{3,1,2,0:T(8,128)(2,1)S(1)} %get-tuple-element.54), channel_id=1, source_target_pairs={{1,0},{2,1},{3,2},{4,3},{5,4},{6,5},{7,6},{0,7},{9,8},{10,9},{11,1... | collective-permute-start | bytes 32264 | tf_op jit(solution)/shard_map/ppermute | solution.py:28
  138.7 3.6 fusion.76
  145.0 4.2 %collective-permute-start.11 = (bf16[1,42,1,128]{3,0,2,1:T(2,128)(2,1)S(1)}, bf16[1,42,1,128]{3,0,2,1:T(2,128)(2,1)S(1)}, u32[]{:S(2)}, u32[]{:S(2)}) collective-permute-start(bf16[1,42,1,128]{3,0,2,1:T(2,128)(2,1)S(1)} %get-tuple-element.40), channel_id=1, source_target_pairs={{1,0},{2,1},{3,2},{4,3},{5,4},{6,5},{7,6},{0,7},{9,8},{10,9},{11,1... | collective-permute-start | bytes 32264 | tf_op jit(solution)/shard_map/ppermute | solution.py:28
  150.6 4.5 %collective-permute-start.20 = (bf16[1,1,64,128]{3,0,2,1:T(2,128)(2,1)S(1)}, bf16[1,1,64,128]{3,0,2,1:T(2,128)(2,1)S(1)}, u32[]{:S(2)}, u32[]{:S(2)}) collective-permute-start(bf16[1,1,64,128]{3,0,2,1:T(2,128)(2,1)S(1)} %slice.172), channel_id=1, source_target_pairs={{0,8},{8,16},{16,24},{24,32},{32,40},{40,48},{48,56},{1,9},{9,17},... | collective-permute-start | bytes 49160 | tf_op jit(solution)/shard_map/ppermute | solution.py:25
  158.0 3.0 pad_maximum_fusion.15
  162.5 62.8 %all-reduce.5.cloned.1.call-done = (f32[3,3,128,128]{3,2,1,0:T(8,128)}, f32[3,3,128,128]{3,2,1,0:T(8,128)}, f32[3,3,128,128]{3,2,1,0:T(8,128)}) async-done(((f32[3,3,128,128]{3,2,1,0:T(8,128)}, f32[3,3,128,128]{3,2,1,0:T(8,128)}, f32[3,3,128,128]{3,2,1,0:T(8,128)}), (f32[3,3,128,128]{3,2,1,0:T(8,128)}, f32[3,3,128,128]{3,2,1,0:T(8,128)}, f32[3,3,128,128]{3,2,1,0:T(8,128)})) %all-reduce.5.cloned.1.call-update) | async-done | bytes 1769488 | tf_op jit(solution)/shard_map/psum | solution.py:11
  225.3 89.8 %all-reduce.6 = (bf16[3,3,128,128]{3,2,1,0:T(8,128)(2,1)}, bf16[3,3,128,128]{3,2,1,0:T(8,128)(2,1)}, bf16[3,3,128,128]{3,2,1,0:T(8,128)(2,1)}) all-reduce(f32[3,3,128,128]{3,2,1,0:T(8,128)} %get-tuple-element.15, f32[3,3,128,128]{3,2,1,0:T(8,128)} %get-tuple-element.16, ...), channel_id=1, replica_groups=mesh['dp'=2,'lat'=8,'lon'=8] {'lat'}, use_global_device_ids=true, to_apply=%region_1.2 | all-reduce | flops 442368 | bytes 2654208 | tf_op jit(solution)/shard_map/psum | solution.py:11
  315.2 3.6 copy_dynamic-update-slice_fusion
  324.5 20.9 %fusion.21 = bf16[1,80,128,128]{3,0,2,1:T(2,128)(2,1)S(1)} fusion(bf16[1,80,128,128]{3,2,1,0:T(8,128)(2,1)S(1)} %copy-done.12, bf16[3,3,128,128]{3,2,1,0:T(8,128)(2,1)S(1)} %copy-done.27, bf16[1,42,66,128]{3,0,2,1:T(2,128)(2,1)} %pad_maximum_fusion.15), kind=kOutput, calls=%fused_computation.25 | convolution fusion | flops 758906880 | bytes 6247424 | tf_op jit(solution)/shard_map/conv_general_dilated | solution.py:39
  347.4 3.0 pad_maximum_fusion.14
  350.4 20.8 %fusion.19 = bf16[1,80,128,128]{3,0,2,1:T(2,128)(2,1)S(1)} fusion(bf16[1,80,128,128]{3,2,1,0:T(8,128)(2,1)S(1)} %copy-done.14, bf16[3,3,128,128]{3,2,1,0:T(8,128)(2,1)S(1)} %copy-done.25, bf16[1,42,66,128]{3,0,2,1:T(2,128)(2,1)} %pad_maximum_fusion.14), kind=kOutput, calls=%fused_computation.22 | convolution fusion | flops 758906880 | bytes 6247424 | tf_op jit(solution)/shard_map/conv_general_dilated | solution.py:39
  (212 shorter events, 90.7 us)
Async XLA Ops:
  7.2 218.2 %all-reduce.5.cloned.1.call-start = ((), (), s32[]{:S(2)}) async-start(), calls=%async_computation.6 | async-start | bytes 3538944 | tf_op jit(solution)/shard_map/psum | solution.py:11
  8.0 29.5 %collective-permute-start.1 = (bf16[1,1,128,128]{3,2,1,0:T(8,128)(2,1)S(1)}, bf16[1,1,128,128]{3,2,1,0:T(8,128)(2,1)S(1)}, u32[]{:S(2)}, u32[]{:S(2)}) collective-permute-start(bf16[1,1,128,128]{3,2,1,0:T(8,128)(2,1)S(1)} %get-tuple-element.35), channel_id=1, source_target_pairs={{8,0},{16,8},{24,16},{32,24},{40,32},{48,40},{56,48},{9,1},{17,9},... | collective-permute-start | bytes 98312 | tf_op jit(solution)/shard_map/ppermute | solution.py:28
  10.2 25.0 %collective-permute-start = (bf16[1,1,128,128]{3,2,1,0:T(8,128)(2,1)S(1)}, bf16[1,1,128,128]{3,2,1,0:T(8,128)(2,1)S(1)}, u32[]{:S(2)}, u32[]{:S(2)}) collective-permute-start(bf16[1,1,128,128]{3,2,1,0:T(8,128)(2,1)S(1)} %get-tuple-element.36), channel_id=1, source_target_pairs={{0,8},{8,16},{16,24},{24,32},{32,40},{40,48},{48,56},{1,9},{9,17},... | collective-permute-start | bytes 98312 | tf_op jit(solution)/shard_map/ppermute | solution.py:25
  17.0 25.2 %collective-permute-start.13 = (bf16[1,1,128,128]{3,2,1,0:T(8,128)(2,1)S(1)}, bf16[1,1,128,128]{3,2,1,0:T(8,128)(2,1)S(1)}, u32[]{:S(2)}, u32[]{:S(2)}) collective-permute-start(bf16[1,1,128,128]{3,2,1,0:T(8,128)(2,1)S(1)} %get-tuple-element.33), channel_id=1, source_target_pairs={{8,0},{16,8},{24,16},{32,24},{40,32},{48,40},{56,48},{9,1},{17,9},... | collective-permute-start | bytes 98312 | tf_op jit(solution)/shard_map/ppermute | solution.py:28
  18.9 18.7 %collective-permute-start.12 = (bf16[1,1,128,128]{3,2,1,0:T(8,128)(2,1)S(1)}, bf16[1,1,128,128]{3,2,1,0:T(8,128)(2,1)S(1)}, u32[]{:S(2)}, u32[]{:S(2)}) collective-permute-start(bf16[1,1,128,128]{3,2,1,0:T(8,128)(2,1)S(1)} %get-tuple-element.34), channel_id=1, source_target_pairs={{0,8},{8,16},{16,24},{24,32},{32,40},{40,48},{48,56},{1,9},{9,17},... | collective-permute-start | bytes 98312 | tf_op jit(solution)/shard_map/ppermute | solution.py:25
  42.3 11.2 %collective-permute-start.14 = (bf16[1,82,1,128]{3,2,1,0:T(2,128)(2,1)S(1)}, bf16[1,82,1,128]{3,2,1,0:T(2,128)(2,1)S(1)}, u32[]{:S(2)}, u32[]{:S(2)}) collective-permute-start(bf16[1,82,1,128]{3,2,1,0:T(2,128)(2,1)S(1)} %get-tuple-element.29), channel_id=1, source_target_pairs={{0,1},{1,2},{2,3},{3,4},{4,5},{5,6},{6,7},{7,0},{8,9},{9,10},{10,1... | collective-permute-start | bytes 62984 | tf_op jit(solution)/shard_map/ppermute | solution.py:25
  42.4 11.1 %collective-permute-start.15 = (bf16[1,82,1,128]{3,2,1,0:T(2,128)(2,1)S(1)}, bf16[1,82,1,128]{3,2,1,0:T(2,128)(2,1)S(1)}, u32[]{:S(2)}, u32[]{:S(2)}) collective-permute-start(bf16[1,82,1,128]{3,2,1,0:T(2,128)(2,1)S(1)} %get-tuple-element.30), channel_id=1, source_target_pairs={{1,0},{2,1},{3,2},{4,3},{5,4},{6,5},{7,6},{0,7},{9,8},{10,9},{11,1... | collective-permute-start | bytes 62984 | tf_op jit(solution)/shard_map/ppermute | solution.py:28
  61.5 18.2 %collective-permute-start.4 = (bf16[1,1,64,128]{3,2,1,0:T(8,128)(2,1)S(1)}, bf16[1,1,64,128]{3,2,1,0:T(8,128)(2,1)S(1)}, u32[]{:S(2)}, u32[]{:S(2)}) collective-permute-start(bf16[1,1,64,128]{3,2,1,0:T(8,128)(2,1)S(1)} %slice.150), channel_id=1, source_target_pairs={{0,8},{8,16},{16,24},{24,32},{32,40},{40,48},{48,56},{1,9},{9,17},... | collective-permute-start | bytes 49160 | tf_op jit(solution)/shard_map/ppermute | solution.py:25
  64.0 15.8 %collective-permute-start.5 = (bf16[1,1,64,128]{3,1,2,0:T(2,128)(2,1)S(1)}, bf16[1,1,64,128]{3,1,2,0:T(2,128)(2,1)S(1)}, u32[]{:S(2)}, u32[]{:S(2)}) collective-permute-start(bf16[1,1,64,128]{3,1,2,0:T(2,128)(2,1)S(1)} %slice.153), channel_id=1, source_target_pairs={{8,0},{16,8},{24,16},{32,24},{40,32},{48,40},{56,48},{9,1},{17,9},... | collective-permute-start | bytes 49160 | tf_op jit(solution)/shard_map/ppermute | solution.py:28
  80.6 10.5 %collective-permute-start.6 = (bf16[1,42,1,128]{3,1,2,0:T(8,128)(2,1)S(1)}, bf16[1,42,1,128]{3,1,2,0:T(8,128)(2,1)S(1)}, u32[]{:S(2)}, u32[]{:S(2)}) collective-permute-start(bf16[1,42,1,128]{3,1,2,0:T(8,128)(2,1)S(1)} %get-tuple-element.55), channel_id=1, source_target_pairs={{0,1},{1,2},{2,3},{3,4},{4,5},{5,6},{6,7},{7,0},{8,9},{9,10},{10,1... | collective-permute-start | bytes 32264 | tf_op jit(solution)/shard_map/ppermute | solution.py:25
  80.7 10.5 %collective-permute-start.7 = (bf16[1,42,1,128]{3,1,2,0:T(8,128)(2,1)S(1)}, bf16[1,42,1,128]{3,1,2,0:T(8,128)(2,1)S(1)}, u32[]{:S(2)}, u32[]{:S(2)}) collective-permute-start(bf16[1,42,1,128]{3,1,2,0:T(8,128)(2,1)S(1)} %get-tuple-element.56), channel_id=1, source_target_pairs={{1,0},{2,1},{3,2},{4,3},{5,4},{6,5},{7,6},{0,7},{9,8},{10,9},{11,1... | collective-permute-start | bytes 32264 | tf_op jit(solution)/shard_map/ppermute | solution.py:28
  103.6 38.8 %collective-permute-start.8 = (bf16[1,1,64,128]{3,0,2,1:T(2,128)(2,1)}, bf16[1,1,64,128]{3,0,2,1:T(2,128)(2,1)}, u32[]{:S(2)}, u32[]{:S(2)}) collective-permute-start(bf16[1,1,64,128]{3,0,2,1:T(2,128)(2,1)} %slice.156), channel_id=1, source_target_pairs={{0,8},{8,16},{16,24},{24,32},{32,40},{40,48},{48,56},{1,9},{9,17},... | collective-permute-start | bytes 49160 | tf_op jit(solution)/shard_map/ppermute | solution.py:25
  106.9 37.8 %collective-permute-start.9 = (bf16[1,1,64,128]{3,0,2,1:T(2,128)(2,1)}, bf16[1,1,64,128]{3,0,2,1:T(2,128)(2,1)S(1)}, u32[]{:S(2)}, u32[]{:S(2)}) collective-permute-start(bf16[1,1,64,128]{3,0,2,1:T(2,128)(2,1)} %slice.159), channel_id=1, source_target_pairs={{8,0},{16,8},{24,16},{32,24},{40,32},{48,40},{56,48},{9,1},{17,9},... | collective-permute-start | bytes 49160 | tf_op jit(solution)/shard_map/ppermute | solution.py:28
  112.2 16.7 %collective-permute-start.16 = (bf16[1,1,64,128]{3,2,1,0:T(8,128)(2,1)}, bf16[1,1,64,128]{3,2,1,0:T(8,128)(2,1)S(1)}, u32[]{:S(2)}, u32[]{:S(2)}) collective-permute-start(bf16[1,1,64,128]{3,2,1,0:T(8,128)(2,1)} %slice.166), channel_id=1, source_target_pairs={{0,8},{8,16},{16,24},{24,32},{32,40},{40,48},{48,56},{1,9},{9,17},... | collective-permute-start | bytes 49160 | tf_op jit(solution)/shard_map/ppermute | solution.py:25
  115.9 13.1 %collective-permute-start.17 = (bf16[1,1,64,128]{3,1,2,0:T(2,128)(2,1)S(1)}, bf16[1,1,64,128]{3,1,2,0:T(2,128)(2,1)S(1)}, u32[]{:S(2)}, u32[]{:S(2)}) collective-permute-start(bf16[1,1,64,128]{3,1,2,0:T(2,128)(2,1)S(1)} %slice.169), channel_id=1, source_target_pairs={{8,0},{16,8},{24,16},{32,24},{40,32},{48,40},{56,48},{9,1},{17,9},... | collective-permute-start | bytes 49160 | tf_op jit(solution)/shard_map/ppermute | solution.py:28
  142.4 230.9 %reduce-scatter.8.cloned.1.call-start = ((), (), s32[]{:S(2)}) async-start(), calls=%async_computation.5 | async-start | bytes 442368 | tf_op jit(solution)/shard_map/reduce_scatter | solution.py:122
  144.8 13.2 %collective-permute-start.10 = (bf16[1,42,1,128]{3,0,2,1:T(2,128)(2,1)S(1)}, bf16[1,42,1,128]{3,0,2,1:T(2,128)(2,1)S(1)}, u32[]{:S(2)}, u32[]{:S(2)}) collective-permute-start(bf16[1,42,1,128]{3,0,2,1:T(2,128)(2,1)S(1)} %get-tuple-element.39), channel_id=1, source_target_pairs={{0,1},{1,2},{2,3},{3,4},{4,5},{5,6},{6,7},{7,0},{8,9},{9,10},{10,1... | collective-permute-start | bytes 32264 | tf_op jit(solution)/shard_map/ppermute | solution.py:25
  145.0 13.0 %collective-permute-start.11 = (bf16[1,42,1,128]{3,0,2,1:T(2,128)(2,1)S(1)}, bf16[1,42,1,128]{3,0,2,1:T(2,128)(2,1)S(1)}, u32[]{:S(2)}, u32[]{:S(2)}) collective-permute-start(bf16[1,42,1,128]{3,0,2,1:T(2,128)(2,1)S(1)} %get-tuple-element.40), channel_id=1, source_target_pairs={{1,0},{2,1},{3,2},{4,3},{5,4},{6,5},{7,6},{0,7},{9,8},{10,9},{11,1... | collective-permute-start | bytes 32264 | tf_op jit(solution)/shard_map/ppermute | solution.py:28
  150.6 11.3 %collective-permute-start.20 = (bf16[1,1,64,128]{3,0,2,1:T(2,128)(2,1)S(1)}, bf16[1,1,64,128]{3,0,2,1:T(2,128)(2,1)S(1)}, u32[]{:S(2)}, u32[]{:S(2)}) collective-permute-start(bf16[1,1,64,128]{3,0,2,1:T(2,128)(2,1)S(1)} %slice.172), channel_id=1, source_target_pairs={{0,8},{8,16},{16,24},{24,32},{32,40},{40,48},{48,56},{1,9},{9,17},... | collective-permute-start | bytes 49160 | tf_op jit(solution)/shard_map/ppermute | solution.py:25
  155.1 163.6 %collective-permute-start.21 = (bf16[1,1,64,128]{3,0,2,1:T(2,128)(2,1)S(1)}, bf16[1,1,64,128]{3,0,2,1:T(2,128)(2,1)S(1)}, u32[]{:S(2)}, u32[]{:S(2)}) collective-permute-start(bf16[1,1,64,128]{3,0,2,1:T(2,128)(2,1)S(1)} %slice.175), channel_id=1, source_target_pairs={{8,0},{16,8},{24,16},{32,24},{40,32},{48,40},{56,48},{9,1},{17,9},... | collective-permute-start | bytes 49160 | tf_op jit(solution)/shard_map/ppermute | solution.py:28
  315.1 59.8 %reduce-scatter.6.cloned.1.call-start = ((), (), s32[]{:S(2)}) async-start(), calls=%async_computation.4 | async-start | bytes 442368 | tf_op jit(solution)/shard_map/reduce_scatter | solution.py:119
  320.2 27.2 %collective-permute-start.22 = (bf16[1,42,1,128]{3,0,2,1:T(2,128)(2,1)S(1)}, bf16[1,42,1,128]{3,0,2,1:T(2,128)(2,1)S(1)}, u32[]{:S(2)}, u32[]{:S(2)}) collective-permute-start(bf16[1,42,1,128]{3,0,2,1:T(2,128)(2,1)S(1)} %get-tuple-element.37), channel_id=1, source_target_pairs={{0,1},{1,2},{2,3},{3,4},{4,5},{5,6},{6,7},{7,0},{8,9},{9,10},{10,1... | collective-permute-start | bytes 32264 | tf_op jit(solution)/shard_map/ppermute | solution.py:25
  322.7 24.7 %collective-permute-start.23 = (bf16[1,42,1,128]{3,0,2,1:T(2,128)(2,1)S(1)}, bf16[1,42,1,128]{3,0,2,1:T(2,128)(2,1)S(1)}, u32[]{:S(2)}, u32[]{:S(2)}) collective-permute-start(bf16[1,42,1,128]{3,0,2,1:T(2,128)(2,1)S(1)} %get-tuple-element.38), channel_id=1, source_target_pairs={{1,0},{2,1},{3,2},{4,3},{5,4},{6,5},{7,6},{0,7},{9,8},{10,9},{11,1... | collective-permute-start | bytes 32264 | tf_op jit(solution)/shard_map/ppermute | solution.py:28
  324.4 52.2 %reduce-scatter.4.cloned.1.call-start = ((), (), s32[]{:S(2)}) async-start(), calls=%async_computation.3 | async-start | bytes 442368 | tf_op jit(solution)/shard_map/reduce_scatter | solution.py:116
  (36 other events, 475.0 us)
Sparse Core Ops, SparseCore 0:
  142.5 82.7 all-reduce.4
  315.2 11.4 reduce-scatter.7
  329.7 11.7 reduce-scatter.5
  350.5 9.7 reduce-scatter.3
